TPU v7x, 32 devices: a whole 2x2x4 slice. The times are simulated.
32 devices in a mesh: groups: 2 (over y), blk: 4 (over z), side: 2 (over x), tp: 2 (over core).
Axes of the slice: x: 2, y: 2, z: 4, core: 2. Of those that a mesh axis runs over, the one named last changes fastest.
Arguments:
- queries: bfloat16 [4, 512, 4096], P(('groups', 'side'), 'blk', 'tp'), parts along dimension 0, may hold values from -8 to 8
- key_rows: bfloat16 [4, 512, 256], P(('groups', 'side'), 'blk', 'tp'), parts along dimension 0, may hold values from -8 to 8
- value_rows: bfloat16 [4, 512, 256], P(('groups', 'side'), 'blk', 'tp'), parts along dimension 0, may hold values from -6 to 6
- segments: int32 [4, 512], P(('groups', 'side'), 'blk'), parts along dimension 0, may hold values from 0 to 1, never falling along the last dimension, each value on 1 to 384 neighbouring positions
- hidden_entry_rows: bfloat16 [4, 512, 4096], P(('groups', 'side'), 'blk', 'tp'), parts along dimension 0, may hold values from -6 to 6
- expert_ids: int32 [4, 512, 8], P(('groups', 'side'), 'blk'), parts along dimension 0, may hold values from 0 to 127, all different within a row; in each aligned block of 128 rows (0 to 127, 128 to 255, ..., all dimensions but the last counted through in order) at most 10 rows name the same one
- route_weight: float32 [4, 512, 8], P(('groups', 'side'), 'blk'), parts along dimension 0, may hold values from 0.2 to 1
- w_gate: bfloat16 [4, 2048, 1536], P('blk', 'tp', 'side'), may hold values from -0.09375 to 0.09375
- w_up: bfloat16 [4, 2048, 1536], P('blk', 'tp', 'side'), may hold values from -0.09375 to 0.09375
- w_down: bfloat16 [4, 1536, 2048], P('blk', 'side', 'tp'), may hold values from -0.15625 to 0.15625
Outputs:
- attended: bfloat16 [4, 512, 4096], P(('groups', 'side'), 'blk', 'tp'), parts along dimension 0
- moe_out: bfloat16 [4, 512, 4096], P(('groups', 'side'), 'blk', 'tp'), parts along dimension 0
There are 2 independent parts, one for each index of `groups`. A program takes and returns all parts, laid end to end along the dimension named above; an argument that names none is the same for every part. Nothing has to cross between parts.
Inputs may be any that keep to these rules, and one draw needn't show every extreme that they name: `expert_ids`: in the 128 rows of one device (aligned blocks of rows of a sequence) no expert is named by more than 10 rows, and in some such block one is named by exactly 10; a row names 8 different experts. `segments`: document numbers never fall along a sequence; a document spans at most 384 positions, and one spans exactly that many.
All inputs are finite; a program needn't handle non-finite values.
Results may differ from a plain program's by a relative error of at most 0.02.
Values may be sent and summed in bfloat16 or wider, within the bound.
A program may use at most 64 MiB of HBM per device.

v0:
```python
import math
import jax
import jax.numpy as jnp
from jax import lax
from jax.sharding import PartitionSpec as P

HEAD_DIM = 128
CAP = 10


def passed_along(value, axis, steps):
    count = lax.axis_size(axis)
    pairs = [(source, (source + steps) % count) for source in range(count)]
    return lax.ppermute(value, axis, pairs)


def slot_choice(id_rows, experts, capacity):
    named = id_rows[:, :, None] == jnp.arange(experts, dtype=jnp.int32)[None, None, :]
    hits = jnp.sum(named.astype(jnp.int32), axis=1)
    ranks = jnp.cumsum(hits, axis=0) - hits
    levels = jnp.arange(capacity, dtype=jnp.int32)[None, :, None]
    return (hits.T[:, None, :] > 0) & (ranks.T[:, None, :] == levels)


def routing_slot_index(id_rows, experts, capacity):
    chosen = slot_choice(id_rows, experts, capacity)
    row_iota = jnp.arange(id_rows.shape[0], dtype=jnp.int32)
    index = jnp.sum(jnp.where(chosen, row_iota[None, None, :], 0), axis=2)
    valid = jnp.any(chosen, axis=2)
    return (index, valid)


def pick_rows(rows, index, valid):
    taken = jnp.take(rows, index, axis=0)
    return jnp.where(valid[..., None], taken, jnp.zeros((), rows.dtype))


def slot_weights(id_rows, weight_rows, experts, capacity):
    named = id_rows[:, :, None] == jnp.arange(experts, dtype=jnp.int32)[None, None, :]
    shares = jnp.sum(jnp.where(named, weight_rows[:, :, None], 0.0), axis=1)
    chosen = slot_choice(id_rows, experts, capacity)
    return chosen.astype(jnp.float32) * shares.T[:, None, :]


def body(
    queries,
    key_rows,
    value_rows,
    segments,
    hidden_entry_rows,
    expert_ids,
    route_weight,
    w_gate,
    w_up,
    w_down,
):
    length = queries.shape[1]
    head_size = HEAD_DIM
    kv_here = key_rows.shape[2] // head_size
    group = queries.shape[2] // (head_size * kv_here)
    query_portion = queries[0].reshape(length, kv_here, group, head_size)
    local_segment_labels = segments[0]
    query_pos = lax.axis_index("blk") * length + jnp.arange(length, dtype=jnp.int32)
    factor = 1.0 / math.sqrt(head_size)
    start_state = (
        jnp.full((length, kv_here, group), -1e30, jnp.float32),
        jnp.zeros((length, kv_here, group), jnp.float32),
        jnp.zeros((length, kv_here, group, head_size), jnp.float32),
    )
    key_piece = lax.all_gather(key_rows[0], "blk", axis=0, tiled=True)
    value_fragment = lax.all_gather(value_rows[0], "blk", axis=0, tiled=True)
    segment_piece = lax.all_gather(local_segment_labels, "blk", axis=0, tiled=True)
    rows_in = key_piece.shape[0]
    width = math.gcd(rows_in, 512)

    def one_block(block_index, state):
        row_max, totals, accumulated = state
        begin = block_index * width
        key_tile_block = lax.dynamic_slice_in_dim(key_piece, begin, width, 0).reshape(
            width, kv_here, head_size
        )
        value_block = lax.dynamic_slice_in_dim(value_fragment, begin, width, 0).reshape(
            width, kv_here, head_size
        )
        segment_block = lax.dynamic_slice_in_dim(segment_piece, begin, width, 0)
        key_pos = begin + jnp.arange(width, dtype=jnp.int32)
        allowed = (key_pos[None, :] <= query_pos[:, None]) & (
            segment_block[None, :] == local_segment_labels[:, None]
        )
        masking = allowed[:, None, None, :]
        scores = (
            jnp.einsum(
                "wsmz,usz->wsmu", query_portion, key_tile_block, preferred_element_type=jnp.float32
            )
            * factor
        )
        scores = jnp.where(masking, scores, -1e30)
        new_max = jnp.maximum(row_max, jnp.max(scores, axis=3))
        rescale = jnp.exp(row_max - new_max)
        weights = jnp.where(masking, jnp.exp(scores - new_max[..., None]), 0.0)
        totals = totals * rescale + jnp.sum(weights, axis=3)
        update = jnp.einsum(
            "jzre,ezm->jzrm",
            weights.astype(jnp.bfloat16),
            value_block,
            preferred_element_type=jnp.float32,
        )
        accumulated = accumulated * rescale[..., None] + update
        return (new_max, totals, accumulated)

    row_max, totals, accumulated = lax.fori_loop(0, rows_in // width, one_block, start_state)
    attended = (
        (accumulated / totals[..., None])
        .astype(jnp.bfloat16)
        .reshape(1, length, group * kv_here * head_size)
    )
    experts = lax.axis_size("blk") // 2
    capacity = CAP
    ff_here = w_gate.shape[2]
    quarter = hidden_entry_rows.shape[2] // 2
    index, valid = routing_slot_index(expert_ids[0], experts, capacity)
    taken = pick_rows(hidden_entry_rows[0], index, valid)
    outgoing = (
        taken.reshape(experts, capacity, 2, quarter)
        .transpose(2, 0, 1, 3)
        .reshape(2 * experts, capacity, quarter)[:, None]
    )
    arrived = lax.all_to_all(outgoing, "blk", split_axis=0, concat_axis=0, tiled=True)
    shards = lax.all_gather(arrived, "side", axis=1, tiled=True)
    gate_piece = jnp.einsum("bscd,df->bscf", shards, w_gate[0], preferred_element_type=jnp.float32)
    up_piece = jnp.einsum("bscd,df->bscf", shards, w_up[0], preferred_element_type=jnp.float32)
    projected = jnp.concatenate([gate_piece, up_piece], axis=3)
    gate_part = projected[..., :ff_here]
    up_part = projected[..., ff_here:]
    gate_sum, up_sum = (
        lax.psum(gate_part.astype(jnp.bfloat16), "tp").astype(jnp.float32),
        lax.psum(up_part.astype(jnp.bfloat16), "tp").astype(jnp.float32),
    )
    both_sums = jnp.stack([gate_sum, up_sum])
    partner_sums = passed_along(
        both_sums.astype(jnp.bfloat16), "blk", lax.axis_size("blk") // 2
    ).astype(both_sums.dtype)
    full_sums = both_sums + partner_sums
    hidden = (jax.nn.silu(full_sums[0]) * full_sums[1]).astype(jnp.bfloat16)
    part_out = jnp.einsum(
        "bscf,fd->bscd", hidden, w_down[0], preferred_element_type=jnp.float32
    ).astype(jnp.bfloat16)
    parts = lax.all_to_all(part_out, "side", split_axis=1, concat_axis=1, tiled=True)
    slot_out = jnp.sum(parts, axis=1, dtype=jnp.float32).astype(jnp.bfloat16)
    returned = lax.all_to_all(slot_out, "blk", split_axis=0, concat_axis=0, tiled=True)
    returned_split = returned.astype(jnp.float32).reshape(2, experts, capacity, quarter)
    own_weighted = slot_weights(expert_ids[0], route_weight[0], experts, capacity)
    mixed = jnp.einsum(
        "ecr,kecq->rkq", own_weighted, returned_split, precision=lax.Precision.HIGHEST
    )
    moe_out = mixed.reshape(mixed.shape[0], 2 * quarter).astype(jnp.bfloat16)[None]
    return (attended, moe_out)


def solution(mesh):
    placed = (
        P(("groups", "side"), "blk", "tp"),
        P(("groups", "side"), "blk", "tp"),
        P(("groups", "side"), "blk", "tp"),
        P(("groups", "side"), "blk"),
        P(("groups", "side"), "blk", "tp"),
        P(("groups", "side"), "blk", None),
        P(("groups", "side"), "blk", None),
        P("blk", "tp", "side"),
        P("blk", "tp", "side"),
        P("blk", "side", "tp"),
    )
    return jax.shard_map(
        body,
        mesh=mesh,
        in_specs=placed,
        out_specs=(P(("groups", "side"), "blk", "tp"), P(("groups", "side"), "blk", "tp")),
        check_vma=False,
    )
```

profile of v0, /device:TPU:0, one launch (start us, length us, event | category | flops | bytes accessed | tf_op | source)
XLA Modules:
  0.0 131.0 jit_solution(2119913399250369770)
XLA Ops:
  7.2 0.0 copy-start
  7.2 0.8 convert_reduce_fusion
  8.0 0.1 copy.47
  8.1 0.2 reduce_window_sum.12
  8.3 0.1 copy.49
  8.4 0.1 select_reduce_fusion
  8.5 0.1 fusion.50
  8.6 0.1 reshape.152
  8.7 1.8 %gather_fusion = bf16[20,2048]{1,0:T(8,128)(2,1)S(1)} fusion(bf16[128,2048]{1,0:T(8,128)(2,1)} %bitcast.124, s32[1024]{0:T(1024)S(1)} %pad_clamp_fusion), kind=kCustom, calls=%fused_computation | custom fusion | bytes 163920 | tf_op jit(solution)/shard_map/jit(_take)/gather | solution.py:34
  10.6 0.7 fusion.47
  11.3 6.3 %all-to-all-start = ((bf16[4,1,10,1024]{3,2,1,0:T(8,128)(2,1)}), bf16[4,1,10,1024]{3,2,1,0:T(8,128)(2,1)S(1)}, u32[]{:S(2)}, u32[]{:S(2)}) async-start(bf16[4,1,10,1024]{3,2,1,0:T(8,128)(2,1)} %bitcast.21), calls=%async_computation | async-start | bytes 262144 | tf_op jit(solution)/shard_map/all_to_all | solution.py:128
  17.7 0.0 all-reduce.3.cloned.1.call-start
  17.7 11.5 %all-gather = s32[1,512]{1,0:T(1,128)S(1)} all-gather(s32[1,128]{1,0:T(1,128)} %param.13), channel_id=2, replica_groups=mesh['groups'=2,'blk'=4,'side'=2,'tp'=2] {'blk'}, dimensions={1}, use_global_device_ids=true | all-gather | bytes 2560 | tf_op jit(solution)/shard_map/all_gather | solution.py:72
  29.2 0.8 fusion.41
  30.0 1.1 copy.62
  31.2 13.6 %all-gather.1 = bf16[1,512,128]{2,1,0:T(8,128)(2,1)S(1)} all-gather(bf16[1,128,128]{2,1,0:T(8,128)(2,1)} %param.11), channel_id=3, replica_groups=mesh['groups'=2,'blk'=4,'side'=2,'tp'=2] {'blk'}, dimensions={1}, use_global_device_ids=true | all-gather | bytes 163840 | tf_op jit(solution)/shard_map/all_gather | solution.py:70
  44.8 0.0 all-to-all-done
  44.8 5.6 %all_gather.15 = bf16[4,2,10,1024]{3,2,1,0:T(8,128)(2,1)S(1)} all-gather(bf16[4,1,10,1024]{3,2,1,0:T(8,128)(2,1)S(1)} %all-to-all-done), channel_id=1, replica_groups=mesh['groups'=2,'blk'=4,'side'=2,'tp'=2] {'side'}, dimensions={1}, use_global_device_ids=true | all-gather | bytes 245760 | tf_op jit(solution)/shard_map/all_gather | solution.py:129
  50.4 2.5 %fusion.33 = bf16[1,4,2,10,768]{4,3,2,1,0:T(8,128)(2,1)} fusion(bf16[4,2,10,1024]{3,2,1,0:T(8,128)(2,1)S(1)} %all_gather.15, bf16[1,1024,768]{2,1,0:T(8,128)(2,1)} %param.17), kind=kOutput, calls=%fused_computation.24 | convolution fusion | flops 125890560 | bytes 1859584 | tf_op jit(solution)/shard_map/bscd,df->bscf/dot_general | solution.py:130
  52.8 2.5 %fusion.30 = bf16[1,4,2,10,768]{4,3,2,1,0:T(8,128)(2,1)} fusion(bf16[4,2,10,1024]{3,2,1,0:T(8,128)(2,1)S(1)} %all_gather.15, bf16[1,1024,768]{2,1,0:T(8,128)(2,1)} %param.18), kind=kOutput, calls=%fused_computation.23 | convolution fusion | flops 125890560 | bytes 1859584 | tf_op jit(solution)/shard_map/bscd,df->bscf/dot_general | solution.py:131
  55.3 0.0 all-reduce.3.cloned.1.call-update
  55.3 2.7 %fusion = (f32[128,16]{0,1:T(8,128)S(1)}, f32[512,128,16]{1,0,2:T(8,128)}) fusion(pred[128,512]{0,1:T(8,128)(4,1)S(1)} %fusion.41, bf16[128,16,128]{2,1,0:T(8,128)(2,1)S(1)} %bitcast.123, bf16[1,512,128]{2,1,0:T(8,128)(2,1)S(1)} %all-gather.1), kind=kOutput, calls=%fused_computation.3 | convolution fusion | flops 271579136 | bytes 4923392 | tf_op jit(solution)/shard_map/while/body/eval_jaxpr/wsmz,usz->wsmu/dot_general | solution.py:92
  58.0 14.2 %all-reduce.3.cloned.1.call-done = (bf16[1,4,2,10,768]{4,3,2,1,0:T(8,128)(2,1)}, bf16[1,4,2,10,768]{4,3,2,1,0:T(8,128)(2,1)}) async-done(((bf16[1,4,2,10,768]{4,3,2,1,0:T(8,128)(2,1)}, bf16[1,4,2,10,768]{4,3,2,1,0:T(8,128)(2,1)}), (bf16[1,4,2,10,768]{4,3,2,1,0:T(8,128)(2,1)}, bf16[1,4,2,10,768]{4,3,2,1,0:T(8,128)(2,1)})) %all-reduce.3.cloned.1.call-update) | async-done | bytes 245776 | tf_op jit(solution)/shard_map/psum | solution.py:136
  72.2 0.9 constant_dynamic-update-slice_fusion.1
  73.2 0.9 constant_dynamic-update-slice_fusion
  74.1 2.8 %collective-permute-start = (bf16[2,4,2,10,768]{4,3,2,1,0:T(8,128)(2,1)S(1)}, bf16[2,4,2,10,768]{4,3,2,1,0:T(8,128)(2,1)S(1)}, u32[]{:S(2)}, u32[]{:S(2)}) collective-permute-start(bf16[2,4,2,10,768]{4,3,2,1,0:T(8,128)(2,1)S(1)} %constant_dynamic-update-slice_fusion), channel_id=1, source_target_pairs={{0,8},{4,12},{8,0},{12,4},{1,9},{5,13},{9,1},{13,5},{2,10},{6,14},... | collective-permute-start | bytes 737288 | tf_op jit(solution)/shard_map/ppermute | solution.py:14
  76.9 0.0 copy-start.1
  76.9 3.2 %fusion.1 = f32[128,16]{0,1:T(8,128)S(1)} fusion(f32[512,128,16]{1,0,2:T(8,128)} %get-tuple-element.48, f32[128,16]{0,1:T(8,128)S(1)} %broadcast_maximum_fusion, pred[128,512]{0,1:T(8,128)(4,1)S(1)} %fusion.41), kind=kLoop, calls=%fused_computation.4 | loop fusion | flops 5240832 | bytes 4276224 | tf_op jit(solution)/shard_map/while/body/eval_jaxpr/reduce_sum | solution.py:101
  80.1 14.7 %collective-permute-done = bf16[2,4,2,10,768]{4,3,2,1,0:T(8,128)(2,1)S(1)} collective-permute-done((bf16[2,4,2,10,768]{4,3,2,1,0:T(8,128)(2,1)S(1)}, bf16[2,4,2,10,768]{4,3,2,1,0:T(8,128)(2,1)S(1)}, u32[]{:S(2)}, u32[]{:S(2)}) %collective-permute-start) | collective-permute-done | bytes 245792 | tf_op jit(solution)/shard_map/ppermute | solution.py:14
  94.8 0.1 convert_add_fusion
  94.9 0.0 copy-done
  95.0 0.4 fusion.21
  95.4 0.8 copy.51
  96.2 3.4 %all-to-all-start.1 = ((bf16[4,2,10,1024]{3,0,2,1:T(4,128)(2,1)}), bf16[4,2,10,1024]{3,0,2,1:T(4,128)(2,1)S(1)}, u32[]{:S(2)}, u32[]{:S(2)}) async-start(bf16[4,2,10,1024]{3,0,2,1:T(4,128)(2,1)} %copy.51), calls=%async_computation.1 | async-start | bytes 327680 | tf_op jit(solution)/shard_map/all_to_all | solution.py:148
  99.6 0.0 copy-done.1
  99.6 0.1 copy.45
  99.8 12.3 %all-gather.2 = bf16[1,512,128]{1,2,0:T(8,128)(2,1)S(1)} all-gather(bf16[1,128,128]{1,2,0:T(8,128)(2,1)S(1)} %copy.45), channel_id=4, replica_groups=mesh['groups'=2,'blk'=4,'side'=2,'tp'=2] {'blk'}, dimensions={1}, use_global_device_ids=true | all-gather | bytes 163840 | tf_op jit(solution)/shard_map/all_gather | solution.py:71
  112.0 0.0 all-to-all-done.1
  112.0 0.1 reduce_sum.60
  112.1 0.7 copy.61
  112.8 3.9 %all-to-all-start.2 = ((bf16[4,10,1024]{2,1,0:T(8,128)(2,1)}), bf16[4,10,1024]{2,1,0:T(8,128)(2,1)S(1)}, u32[]{:S(2)}, u32[]{:S(2)}) async-start(bf16[4,10,1024]{2,1,0:T(8,128)(2,1)} %copy.61), calls=%async_computation.2 | async-start | bytes 262144 | tf_op jit(solution)/shard_map/all_to_all | solution.py:150
  116.7 0.0 copy-start.2
  116.7 0.0 copy-start.3
  116.7 3.4 %divide_convert_fusion = bf16[1,128,128,16]{2,1,3,0:T(8,128)(2,1)S(1)} fusion(f32[512,128,16]{1,0,2:T(8,128)} %get-tuple-element.48, f32[128,16]{0,1:T(8,128)S(1)} %broadcast_maximum_fusion, pred[128,512]{0,1:T(8,128)(4,1)S(1)} %fusion.41, f32[128,16]{0,1:T(8,128)S(1)} %get-tuple-element.46, f32[128,16]{0,1:T(8,128)S(1)} %get-tuple-element.45, ...), kind=kOutput, calls=%fused_computation.25 | convolution fusion | flops 274464768 | bytes 4939776 | tf_op jit(solution)/shard_map/while/body/eval_jaxpr/jzre,ezm->jzrm/dot_general | solution.py:102
  120.1 1.0 copy.55
  121.1 0.0 copy-done.2
  121.1 0.0 copy-done.3
  121.1 1.4 %all-to-all-done.2 = bf16[4,10,1024]{2,1,0:T(8,128)(2,1)S(1)} async-done(((bf16[4,10,1024]{2,1,0:T(8,128)(2,1)}), bf16[4,10,1024]{2,1,0:T(8,128)(2,1)S(1)}, u32[]{:S(2)}, u32[]{:S(2)}) %all-to-all-start.2) | async-done | bytes 81952 | tf_op jit(solution)/shard_map/all_to_all | solution.py:150
  122.6 0.1 copy.60
  122.7 1.4 %fusion.4 = bf16[1,128,2048]{2,1,0:T(8,128)(2,1)} fusion(bf16[2048,10,2]{0,2,1:T(2,128)(2,1)S(1)} %bitcast.125, f32[2,128]{1,0:T(2,128)S(1)} %bitcast.132, s32[2,128]{1,0:T(2,128)S(1)} %copy.49, pred[2,128]{1,0:T(4,128)(4,1)S(1)} %compare_bitcast_fusion), kind=kOutput, calls=%fused_computation.8 | convolution fusion | flops 63184384 | bytes 608512 | tf_op jit(solution)/shard_map/ecr,kecq->rkq/dot_general | solution.py:153
  (10 shorter events, 0.1 us)
Async XLA Ops:
  7.2 87.8 %copy-start = (bf16[1,768,1024]{2,1,0:T(8,128)(2,1)S(1)}, bf16[1,768,1024]{2,1,0:T(8,128)(2,1)}, u32[]{:S(2)}) copy-start(bf16[1,768,1024]{2,1,0:T(8,128)(2,1)} %param.19) | copy-start | bytes 4718596
  11.3 33.4 %all-to-all-start = ((bf16[4,1,10,1024]{3,2,1,0:T(8,128)(2,1)}), bf16[4,1,10,1024]{3,2,1,0:T(8,128)(2,1)S(1)}, u32[]{:S(2)}, u32[]{:S(2)}) async-start(bf16[4,1,10,1024]{3,2,1,0:T(8,128)(2,1)} %bitcast.21), calls=%async_computation | async-start | bytes 262144 | tf_op jit(solution)/shard_map/all_to_all | solution.py:128
  17.7 54.5 %all-reduce.3.cloned.1.call-start = ((), (), s32[]{:S(2)}) async-start(), calls=%async_computation.3 | async-start | bytes 786432 | tf_op jit(solution)/shard_map/psum | solution.py:136
  74.1 20.7 %collective-permute-start = (bf16[2,4,2,10,768]{4,3,2,1,0:T(8,128)(2,1)S(1)}, bf16[2,4,2,10,768]{4,3,2,1,0:T(8,128)(2,1)S(1)}, u32[]{:S(2)}, u32[]{:S(2)}) collective-permute-start(bf16[2,4,2,10,768]{4,3,2,1,0:T(8,128)(2,1)S(1)} %constant_dynamic-update-slice_fusion), channel_id=1, source_target_pairs={{0,8},{4,12},{8,0},{12,4},{1,9},{5,13},{9,1},{13,5},{2,10},{6,14},... | collective-permute-start | bytes 737288 | tf_op jit(solution)/shard_map/ppermute | solution.py:14
  76.9 22.8 %copy-start.1 = (bf16[1,128,128]{2,1,0:T(8,128)(2,1)S(1)}, bf16[1,128,128]{2,1,0:T(8,128)(2,1)}, u32[]{:S(2)}) copy-start(bf16[1,128,128]{2,1,0:T(8,128)(2,1)} %param.12) | copy-start | bytes 98308
  96.2 15.8 %all-to-all-start.1 = ((bf16[4,2,10,1024]{3,0,2,1:T(4,128)(2,1)}), bf16[4,2,10,1024]{3,0,2,1:T(4,128)(2,1)S(1)}, u32[]{:S(2)}, u32[]{:S(2)}) async-start(bf16[4,2,10,1024]{3,0,2,1:T(4,128)(2,1)} %copy.51), calls=%async_computation.1 | async-start | bytes 327680 | tf_op jit(solution)/shard_map/all_to_all | solution.py:148
  112.8 9.8 %all-to-all-start.2 = ((bf16[4,10,1024]{2,1,0:T(8,128)(2,1)}), bf16[4,10,1024]{2,1,0:T(8,128)(2,1)S(1)}, u32[]{:S(2)}, u32[]{:S(2)}) async-start(bf16[4,10,1024]{2,1,0:T(8,128)(2,1)} %copy.61), calls=%async_computation.2 | async-start | bytes 262144 | tf_op jit(solution)/shard_map/all_to_all | solution.py:150
  116.7 4.4 %copy-start.2 = (s32[1,128,8]{1,2,0:T(8,128)S(1)}, s32[1,128,8]{1,2,0:T(8,128)}, u32[]{:S(2)}) copy-start(s32[1,128,8]{1,2,0:T(8,128)} %param.15) | copy-start | bytes 12292
  116.7 4.5 %copy-start.3 = (f32[1,128,8]{1,2,0:T(8,128)S(1)}, f32[1,128,8]{1,2,0:T(8,128)}, u32[]{:S(2)}) copy-start(f32[1,128,8]{1,2,0:T(8,128)} %param.16) | copy-start | bytes 12292
Sparse Core Ops, SparseCore 0:
  55.4 16.7 all-reduce.2
where the time goes:
time: 132 us; the launch traced here: 131 us
  blocking collectives  43 us (33%)
  waiting for transfers between devices  30.4 us (23%)
  starting transfers between devices  16.4 us (12%)
  between operations  14.2 us (11%)
  matrix products  12.9 us (10%)
  local copies, waits for them, and re-layouts  7.85 us (6%)
  other arithmetic  6.27 us (5%)
    ppermute x1, waiting for transfers between devices, passed_along(): return lax.ppermute(value, axis, pairs)  14.7 us
    psum x1, waiting for transfers between devices, body(): lax.psum(gate_part.astype(jnp.bfloat16), 'tp').astype(jnp.float32)  14.2 us
    all_gather x1, blocking collectives, body(): key_piece = lax.all_gather(key_rows[0], 'blk', axis=0, tiled=True)  13.6 us
    all_gather x1, blocking collectives, body(): value_fragment = lax.all_gather(value_rows[0], 'blk', axis=0, tiled=True)  12.3 us
    all_gather x1, blocking collectives, body(): lax.all_gather(local_segment_labels, 'blk', axis=0, tiled=True)  11.5 us
    all_to_all x1, starting transfers between devices, body(): lax.all_to_all(outgoing, 'blk', split_axis=0, concat_axis=0, tiled=True)  6.35 us
    all_gather x1, blocking collectives, body(): shards = lax.all_gather(arrived, 'side', axis=1, tiled=True)  5.63 us
    unnamed x13, local copies, waits for them, and re-layouts  3.93 us
  transfers between devices with their start and end apart: 5, of which 3 were waited for; matrix products, arithmetic and copies ran while one was open for 9% of the time, Pallas kernels for 0%

commit v1 on v0

--- a/solution.py
+++ b/solution.py
@@ -6,6 +6,12 @@
 
 HEAD_DIM = 128
 CAP = 10
+
+
+def laid_out(parts, dim):
+    lengths = list(parts.shape[1:])
+    lengths[dim] *= parts.shape[0]
+    return jnp.moveaxis(parts, 0, dim).reshape(lengths)
 
 
 def passed_along(value, axis, steps):
@@ -69,7 +75,19 @@
     )
     key_piece = lax.all_gather(key_rows[0], "blk", axis=0, tiled=True)
     value_fragment = lax.all_gather(value_rows[0], "blk", axis=0, tiled=True)
-    segment_piece = lax.all_gather(local_segment_labels, "blk", axis=0, tiled=True)
+    size = lax.axis_size("blk")
+    pairs_2 = [(i, (i + 1) % size) for i in range(size)]
+    back = [(b, a) for a, b in pairs_2]
+    lower, upper = ([], [])
+    for step in range(size - 1):
+        if step % 2 == 0:
+            lower.append(lax.ppermute(lower[-1] if lower else local_segment_labels, "blk", pairs_2))
+        else:
+            upper.append(lax.ppermute(upper[-1] if upper else local_segment_labels, "blk", back))
+    pieces = jnp.stack([*lower[::-1], local_segment_labels, *upper])
+    shift = lax.axis_index("blk") - len(lower)
+    pieces = pieces[(jnp.arange(size) - shift) % size]
+    segment_piece = laid_out(pieces, 0)
     rows_in = key_piece.shape[0]
     width = math.gcd(rows_in, 512)
 

time: 132 us -> 135 us (1.023)
  blocking collectives: 43 us -> 32 us
  starting transfers between devices: 16.4 us -> 22.7 us
  waiting for transfers between devices: 30.4 us -> 35.6 us
    all_gather x1 -> x0, blocking collectives: 11.5 us -> none  [body(): lax.all_gather(local_segment_labels, 'blk', axis=0, tiled=True)]
    ppermute x0 -> x3, starting transfers between devices: none -> 6.65 us  [the longest x1 5.13 us: body(): lax.ppermute(upper[-1] if upper else local_segment_labels, 'blk', back)]
    all_to_all x1, waiting for transfers between devices: 0.01 us -> 4.62 us  [body(): lax.all_to_all(part_out, 'side', split_axis=1, concat_axis=1, tiled=True)]
    unnamed x13 -> x7, local copies, waits for them, and re-layouts: 3.93 us -> 4.66 us
  transfers between devices with their start and end apart: 5 -> 8, of which waited for: 3 -> 4; matrix products, arithmetic and copies ran while one was open for 9% -> 14% of each run, Pallas kernels for 0% -> 0%
where the time goes in v1:
time: 135 us; the launch traced here: 134 us
  waiting for transfers between devices  35.6 us (26%)
  blocking collectives  32 us (24%)
  starting transfers between devices  22.7 us (17%)
  between operations  14.2 us (11%)
  matrix products  12.8 us (9%)
  local copies, waits for them, and re-layouts  9.14 us (7%)
  other arithmetic  7.5 us (6%)
    ppermute x1, waiting for transfers between devices, passed_along(): return lax.ppermute(value, axis, pairs)  14.8 us
    psum x1, waiting for transfers between devices, body(): lax.psum(gate_part.astype(jnp.bfloat16), 'tp').astype(jnp.float32)  14.7 us
    all_gather x1, blocking collectives, body(): key_piece = lax.all_gather(key_rows[0], 'blk', axis=0, tiled=True)  14.1 us
    all_gather x1, blocking collectives, body(): value_fragment = lax.all_gather(value_rows[0], 'blk', axis=0, tiled=True)  12.3 us
    all_gather x1, blocking collectives, body(): shards = lax.all_gather(arrived, 'side', axis=1, tiled=True)  5.64 us
    ppermute x1, starting transfers between devices, body(): lax.ppermute(upper[-1] if upper else local_segment_labels, 'blk', back)  5.13 us
    all_to_all x1, starting transfers between devices, body(): lax.all_to_all(outgoing, 'blk', split_axis=0, concat_axis=0, tiled=True)  5.09 us
    all_to_all x1, starting transfers between devices, body(): lax.all_to_all(slot_out, 'blk', split_axis=0, concat_axis=0, tiled=True)  4.81 us
  transfers between devices with their start and end apart: 8, of which 4 were waited for; matrix products, arithmetic and copies ran while one was open for 14% of the time, Pallas kernels for 0%

profile of v1, /device:TPU:0, one launch (start us, length us, event | category | flops | bytes accessed | tf_op | source)
XLA Modules:
  0.0 134.1 jit_solution(9005777975512976800)
XLA Ops:
  7.2 0.0 copy-start
  7.2 5.1 %collective-permute-start.2 = (s32[128]{0:T(128)}, s32[128]{0:T(128)S(1)}, u32[]{:S(2)}, u32[]{:S(2)}) collective-permute-start(s32[128]{0:T(128)} %bitcast.139), channel_id=1, source_target_pairs={{4,0},{8,4},{12,8},{0,12},{5,1},{9,5},{13,9},{1,13},{6,2},{10,6},{... | collective-permute-start | bytes 1544 | tf_op jit(solution)/shard_map/ppermute | solution.py:86
  12.3 0.0 collective-permute-start
  12.3 0.7 convert_reduce_fusion
  13.0 0.1 copy.47
  13.1 0.2 reduce_window_sum.12
  13.3 0.1 copy.49
  13.4 0.1 select_reduce_fusion
  13.5 0.1 fusion.50
  13.7 0.1 reshape.214
  13.8 1.8 %gather_fusion.1 = bf16[20,2048]{1,0:T(8,128)(2,1)S(1)} fusion(bf16[128,2048]{1,0:T(8,128)(2,1)} %bitcast.129, s32[1024]{0:T(1024)S(1)} %pad_clamp_fusion), kind=kCustom, calls=%fused_computation.1 | custom fusion | bytes 163920 | tf_op jit(solution)/shard_map/jit(_take)/gather | solution.py:40
  15.6 0.7 fusion.47
  16.3 5.1 %all-to-all-start = ((bf16[4,1,10,1024]{3,2,1,0:T(8,128)(2,1)}), bf16[4,1,10,1024]{3,2,1,0:T(8,128)(2,1)S(1)}, u32[]{:S(2)}, u32[]{:S(2)}) async-start(bf16[4,1,10,1024]{3,2,1,0:T(8,128)(2,1)} %bitcast.25), calls=%async_computation | async-start | bytes 262144 | tf_op jit(solution)/shard_map/all_to_all | solution.py:146
  21.4 0.0 all-reduce.3.cloned.1.call-start
  21.5 0.7 select_reduce_fusion.1
  22.2 14.1 %all-gather = bf16[1,512,128]{2,1,0:T(8,128)(2,1)S(1)} all-gather(bf16[1,128,128]{2,1,0:T(8,128)(2,1)} %param.11), channel_id=2, replica_groups=mesh['groups'=2,'blk'=4,'side'=2,'tp'=2] {'blk'}, dimensions={1}, use_global_device_ids=true | all-gather | bytes 163840 | tf_op jit(solution)/shard_map/all_gather | solution.py:76
  36.3 0.9 copy.45
  37.2 0.0 collective-permute-done
  37.2 1.5 %collective-permute-start.1 = (s32[128]{0:T(128)S(1)}, s32[128]{0:T(128)S(1)}, u32[]{:S(2)}, u32[]{:S(2)}) collective-permute-start(s32[128]{0:T(128)S(1)} %collective-permute-done), channel_id=1, source_target_pairs={{0,4},{4,8},{8,12},{12,0},{1,5},{5,9},{9,13},{13,1},{2,6},{6,10},{... | collective-permute-start | bytes 1544 | tf_op jit(solution)/shard_map/ppermute | solution.py:84
  38.7 12.3 %all-gather.1 = bf16[1,512,128]{1,2,0:T(8,128)(2,1)S(1)} all-gather(bf16[1,128,128]{1,2,0:T(8,128)(2,1)S(1)} %copy.45), channel_id=3, replica_groups=mesh['groups'=2,'blk'=4,'side'=2,'tp'=2] {'blk'}, dimensions={1}, use_global_device_ids=true | all-gather | bytes 163840 | tf_op jit(solution)/shard_map/all_gather | solution.py:77
  51.0 1.1 copy.62
  52.1 0.0 collective-permute-done.2
  52.1 0.0 collective-permute-done.1
  52.1 0.7 pad_add_fusion
  52.8 0.6 gather_fusion
  53.4 0.8 fusion.41
  54.2 0.0 all-to-all-done
  54.2 5.6 %all_gather.11 = bf16[4,2,10,1024]{3,2,1,0:T(8,128)(2,1)S(1)} all-gather(bf16[4,1,10,1024]{3,2,1,0:T(8,128)(2,1)S(1)} %all-to-all-done), channel_id=1, replica_groups=mesh['groups'=2,'blk'=4,'side'=2,'tp'=2] {'side'}, dimensions={1}, use_global_device_ids=true | all-gather | bytes 245760 | tf_op jit(solution)/shard_map/all_gather | solution.py:147
  59.8 2.5 %fusion.33 = bf16[1,4,2,10,768]{4,3,2,1,0:T(8,128)(2,1)} fusion(bf16[4,2,10,1024]{3,2,1,0:T(8,128)(2,1)S(1)} %all_gather.11, bf16[1,1024,768]{2,1,0:T(8,128)(2,1)} %param.17), kind=kOutput, calls=%fused_computation.25 | convolution fusion | flops 125890560 | bytes 1859584 | tf_op jit(solution)/shard_map/bscd,df->bscf/dot_general | solution.py:148
  62.3 2.5 %fusion.30 = bf16[1,4,2,10,768]{4,3,2,1,0:T(8,128)(2,1)} fusion(bf16[4,2,10,1024]{3,2,1,0:T(8,128)(2,1)S(1)} %all_gather.11, bf16[1,1024,768]{2,1,0:T(8,128)(2,1)} %param.18), kind=kOutput, calls=%fused_computation.24 | convolution fusion | flops 125890560 | bytes 1859584 | tf_op jit(solution)/shard_map/bscd,df->bscf/dot_general | solution.py:149
  64.7 0.0 all-reduce.3.cloned.1.call-update
  64.8 2.7 %fusion = (f32[128,16]{0,1:T(8,128)S(1)}, f32[512,128,16]{1,0,2:T(8,128)}) fusion(pred[128,512]{0,1:T(8,128)(4,1)S(1)} %fusion.41, bf16[128,16,128]{2,1,0:T(8,128)(2,1)S(1)} %bitcast.128, bf16[1,512,128]{2,1,0:T(8,128)(2,1)S(1)} %all-gather), kind=kOutput, calls=%fused_computation.4 | convolution fusion | flops 271579136 | bytes 4923392 | tf_op jit(solution)/shard_map/while/body/eval_jaxpr/wsmz,usz->wsmu/dot_general | solution.py:110
  67.5 14.7 %all-reduce.3.cloned.1.call-done = (bf16[1,4,2,10,768]{4,3,2,1,0:T(8,128)(2,1)}, bf16[1,4,2,10,768]{4,3,2,1,0:T(8,128)(2,1)}) async-done(((bf16[1,4,2,10,768]{4,3,2,1,0:T(8,128)(2,1)}, bf16[1,4,2,10,768]{4,3,2,1,0:T(8,128)(2,1)}), (bf16[1,4,2,10,768]{4,3,2,1,0:T(8,128)(2,1)}, bf16[1,4,2,10,768]{4,3,2,1,0:T(8,128)(2,1)})) %all-reduce.3.cloned.1.call-update) | async-done | bytes 245776 | tf_op jit(solution)/shard_map/psum | solution.py:154
  82.1 0.9 constant_dynamic-update-slice_fusion.1
  83.1 0.9 constant_dynamic-update-slice_fusion
  84.0 2.8 %collective-permute-start.3 = (bf16[2,4,2,10,768]{4,3,2,1,0:T(8,128)(2,1)S(1)}, bf16[2,4,2,10,768]{4,3,2,1,0:T(8,128)(2,1)S(1)}, u32[]{:S(2)}, u32[]{:S(2)}) collective-permute-start(bf16[2,4,2,10,768]{4,3,2,1,0:T(8,128)(2,1)S(1)} %constant_dynamic-update-slice_fusion), channel_id=1, source_target_pairs={{0,8},{4,12},{8,0},{12,4},{1,9},{5,13},{9,1},{13,5},{2,10},{6,14},... | collective-permute-start | bytes 737288 | tf_op jit(solution)/shard_map/ppermute | solution.py:20
  86.8 3.2 %fusion.1 = f32[128,16]{0,1:T(8,128)S(1)} fusion(f32[512,128,16]{1,0,2:T(8,128)} %get-tuple-element.48, f32[128,16]{0,1:T(8,128)S(1)} %broadcast_maximum_fusion, pred[128,512]{0,1:T(8,128)(4,1)S(1)} %fusion.41), kind=kLoop, calls=%fused_computation.5 | loop fusion | flops 5240832 | bytes 4276224 | tf_op jit(solution)/shard_map/while/body/eval_jaxpr/reduce_sum | solution.py:119
  90.0 14.8 %collective-permute-done.3 = bf16[2,4,2,10,768]{4,3,2,1,0:T(8,128)(2,1)S(1)} collective-permute-done((bf16[2,4,2,10,768]{4,3,2,1,0:T(8,128)(2,1)S(1)}, bf16[2,4,2,10,768]{4,3,2,1,0:T(8,128)(2,1)S(1)}, u32[]{:S(2)}, u32[]{:S(2)}) %collective-permute-start.3) | collective-permute-done | bytes 245792 | tf_op jit(solution)/shard_map/ppermute | solution.py:20
  104.8 0.1 convert_add_fusion
  104.9 0.0 copy-done
  104.9 0.4 fusion.21
  105.3 0.8 copy.51
  106.1 3.4 %all-to-all-start.1 = ((bf16[4,2,10,1024]{3,0,2,1:T(4,128)(2,1)}), bf16[4,2,10,1024]{3,0,2,1:T(4,128)(2,1)S(1)}, u32[]{:S(2)}, u32[]{:S(2)}) async-start(bf16[4,2,10,1024]{3,0,2,1:T(4,128)(2,1)} %copy.51), calls=%async_computation.1 | async-start | bytes 327680 | tf_op jit(solution)/shard_map/all_to_all | solution.py:166
  109.6 4.6 %all-to-all-done.1 = bf16[4,2,10,1024]{3,0,2,1:T(4,128)(2,1)S(1)} async-done(((bf16[4,2,10,1024]{3,0,2,1:T(4,128)(2,1)}), bf16[4,2,10,1024]{3,0,2,1:T(4,128)(2,1)S(1)}, u32[]{:S(2)}, u32[]{:S(2)}) %all-to-all-start.1) | async-done | bytes 163872 | tf_op jit(solution)/shard_map/all_to_all | solution.py:166
  114.2 0.1 reduce_sum.60
  114.3 0.7 copy.61
  115.0 4.8 %all-to-all-start.2 = ((bf16[4,10,1024]{2,1,0:T(8,128)(2,1)}), bf16[4,10,1024]{2,1,0:T(8,128)(2,1)S(1)}, u32[]{:S(2)}, u32[]{:S(2)}) async-start(bf16[4,10,1024]{2,1,0:T(8,128)(2,1)} %copy.61), calls=%async_computation.2 | async-start | bytes 262144 | tf_op jit(solution)/shard_map/all_to_all | solution.py:168
  119.8 3.4 %divide_convert_fusion = bf16[1,128,128,16]{2,1,3,0:T(8,128)(2,1)S(1)} fusion(f32[512,128,16]{1,0,2:T(8,128)} %get-tuple-element.48, f32[128,16]{0,1:T(8,128)S(1)} %broadcast_maximum_fusion, pred[128,512]{0,1:T(8,128)(4,1)S(1)} %fusion.41, f32[128,16]{0,1:T(8,128)S(1)} %get-tuple-element.46, f32[128,16]{0,1:T(8,128)S(1)} %get-tuple-element.45, ...), kind=kOutput, calls=%fused_computation.26 | convolution fusion | flops 274464768 | bytes 4939776 | tf_op jit(solution)/shard_map/while/body/eval_jaxpr/jzre,ezm->jzrm/dot_general | solution.py:120
  123.2 1.0 copy.55
  124.2 1.5 %all-to-all-done.2 = bf16[4,10,1024]{2,1,0:T(8,128)(2,1)S(1)} async-done(((bf16[4,10,1024]{2,1,0:T(8,128)(2,1)}), bf16[4,10,1024]{2,1,0:T(8,128)(2,1)S(1)}, u32[]{:S(2)}, u32[]{:S(2)}) %all-to-all-start.2) | async-done | bytes 81952 | tf_op jit(solution)/shard_map/all_to_all | solution.py:168
  125.7 0.1 copy.60
  125.8 1.4 %fusion.4 = bf16[1,128,2048]{2,1,0:T(8,128)(2,1)} fusion(bf16[2048,10,2]{0,2,1:T(2,128)(2,1)S(1)} %bitcast.130, f32[2,128]{1,0:T(2,128)S(1)} %bitcast.137, s32[2,128]{1,0:T(2,128)S(1)} %copy.49, pred[2,128]{1,0:T(4,128)(4,1)S(1)} %compare_bitcast_fusion), kind=kOutput, calls=%fused_computation.9 | convolution fusion | flops 63184384 | bytes 608512 | tf_op jit(solution)/shard_map/ecr,kecq->rkq/dot_general | solution.py:171
  (11 shorter events, 0.1 us)
Async XLA Ops:
  7.2 97.7 %copy-start = (bf16[1,768,1024]{2,1,0:T(8,128)(2,1)S(1)}, bf16[1,768,1024]{2,1,0:T(8,128)(2,1)}, u32[]{:S(2)}) copy-start(bf16[1,768,1024]{2,1,0:T(8,128)(2,1)} %param.19) | copy-start | bytes 4718596
  7.2 45.0 %collective-permute-start.2 = (s32[128]{0:T(128)}, s32[128]{0:T(128)S(1)}, u32[]{:S(2)}, u32[]{:S(2)}) collective-permute-start(s32[128]{0:T(128)} %bitcast.139), channel_id=1, source_target_pairs={{4,0},{8,4},{12,8},{0,12},{5,1},{9,5},{13,9},{1,13},{6,2},{10,6},{... | collective-permute-start | bytes 1544 | tf_op jit(solution)/shard_map/ppermute | solution.py:86
  12.3 24.9 %collective-permute-start = (s32[128]{0:T(128)}, s32[128]{0:T(128)S(1)}, u32[]{:S(2)}, u32[]{:S(2)}) collective-permute-start(s32[128]{0:T(128)} %bitcast.140), channel_id=1, source_target_pairs={{0,4},{4,8},{8,12},{12,0},{1,5},{5,9},{9,13},{13,1},{2,6},{6,10},{... | collective-permute-start | bytes 1544 | tf_op jit(solution)/shard_map/ppermute | solution.py:84
  16.3 37.8 %all-to-all-start = ((bf16[4,1,10,1024]{3,2,1,0:T(8,128)(2,1)}), bf16[4,1,10,1024]{3,2,1,0:T(8,128)(2,1)S(1)}, u32[]{:S(2)}, u32[]{:S(2)}) async-start(bf16[4,1,10,1024]{3,2,1,0:T(8,128)(2,1)} %bitcast.25), calls=%async_computation | async-start | bytes 262144 | tf_op jit(solution)/shard_map/all_to_all | solution.py:146
  21.4 60.7 %all-reduce.3.cloned.1.call-start = ((), (), s32[]{:S(2)}) async-start(), calls=%async_computation.3 | async-start | bytes 786432 | tf_op jit(solution)/shard_map/psum | solution.py:154
  37.2 15.0 %collective-permute-start.1 = (s32[128]{0:T(128)S(1)}, s32[128]{0:T(128)S(1)}, u32[]{:S(2)}, u32[]{:S(2)}) collective-permute-start(s32[128]{0:T(128)S(1)} %collective-permute-done), channel_id=1, source_target_pairs={{0,4},{4,8},{8,12},{12,0},{1,5},{5,9},{9,13},{13,1},{2,6},{6,10},{... | collective-permute-start | bytes 1544 | tf_op jit(solution)/shard_map/ppermute | solution.py:84
  84.0 20.7 %collective-permute-start.3 = (bf16[2,4,2,10,768]{4,3,2,1,0:T(8,128)(2,1)S(1)}, bf16[2,4,2,10,768]{4,3,2,1,0:T(8,128)(2,1)S(1)}, u32[]{:S(2)}, u32[]{:S(2)}) collective-permute-start(bf16[2,4,2,10,768]{4,3,2,1,0:T(8,128)(2,1)S(1)} %constant_dynamic-update-slice_fusion), channel_id=1, source_target_pairs={{0,8},{4,12},{8,0},{12,4},{1,9},{5,13},{9,1},{13,5},{2,10},{6,14},... | collective-permute-start | bytes 737288 | tf_op jit(solution)/shard_map/ppermute | solution.py:20
  106.1 8.1 %all-to-all-start.1 = ((bf16[4,2,10,1024]{3,0,2,1:T(4,128)(2,1)}), bf16[4,2,10,1024]{3,0,2,1:T(4,128)(2,1)S(1)}, u32[]{:S(2)}, u32[]{:S(2)}) async-start(bf16[4,2,10,1024]{3,0,2,1:T(4,128)(2,1)} %copy.51), calls=%async_computation.1 | async-start | bytes 327680 | tf_op jit(solution)/shard_map/all_to_all | solution.py:166
  115.0 10.7 %all-to-all-start.2 = ((bf16[4,10,1024]{2,1,0:T(8,128)(2,1)}), bf16[4,10,1024]{2,1,0:T(8,128)(2,1)S(1)}, u32[]{:S(2)}, u32[]{:S(2)}) async-start(bf16[4,10,1024]{2,1,0:T(8,128)(2,1)} %copy.61), calls=%async_computation.2 | async-start | bytes 262144 | tf_op jit(solution)/shard_map/all_to_all | solution.py:168
Sparse Core Ops, SparseCore 0:
  64.9 17.2 all-reduce.2
